TPU v7x, 512 devices: a whole 4x4x16 slice. The times are simulated.
512 devices in a mesh: ctx: 64 (over x, z), ch: 8 (over y, core).
Axes of the slice: x: 4, y: 4, z: 16, core: 2. Of those that a mesh axis runs over, the one named last changes fastest.
Arguments:
- q_proj: bfloat16 [16384, 4096], P('ctx', 'ch'), may hold values from -6 to 6
- k_proj: bfloat16 [16384, 4096], P('ctx', 'ch'), may hold values from -6 to 6
- v_proj: bfloat16 [16384, 4096], P('ctx', 'ch'), may hold values from -6 to 6
- residue: float32 [16, 4096], P(None, 'ch'), may hold values from -4 to 4
- rate: float32 [16, 4096], P(None, 'ch'), may hold values from 1.2207031e-05 to 0.1
- skip: float32 [4096], P('ch'), may hold values from -4 to 4
- w_out: bfloat16 [4096, 6144], P('ctx', 'ch'), may hold values from -0.09375 to 0.09375
Outputs:
- mixed: bfloat16 [16384, 6144], P('ctx', 'ch')
All inputs are finite; a program needn't handle non-finite values.
Results may differ from a plain program's by a relative error of at most 0.0049.
Values may be sent and summed in bfloat16 or wider, within the bound.
A program may use at most 128 MiB of HBM per device.

v0:
```python
import jax
import jax.numpy as jnp
from jax import lax
from jax.sharding import PartitionSpec as P


def carried_in(part, axis, combine, identity):
    place = lax.axis_index(axis)
    gathered = jax.tree.map(lambda a: lax.all_gather(a, axis), part)
    state = jax.tree.map(lambda a, e: jnp.zeros_like(a) + jnp.asarray(e, a.dtype), part, identity)

    def one(turn, state):
        return combine(
            state, jax.tree.map(lambda a: lax.dynamic_index_in_dim(a, turn, 0, False), gathered)
        )

    return lax.fori_loop(0, place, one, state)


def compose(earlier, later):
    return (earlier[0] * later[0], later[0] * earlier[1] + later[1])


def body(q_proj, k_proj, v_proj, residue, rate, skip, w_out):
    highest = lax.Precision.HIGHEST
    tok_rows, chan_count = q_proj.shape
    signal = k_proj.astype(jnp.float32) * v_proj.astype(jnp.float32)
    sub_len = min(64, tok_rows // 4)
    sub_count = tok_rows // sub_len
    pieces = signal.reshape(sub_count, sub_len, chan_count)
    lag_steps = jnp.arange(sub_len).astype(jnp.float32)
    powers = jnp.exp(-rate[:, None, :] * lag_steps[None, :, None])
    coefficient = residue * jnp.sqrt(2.0 * rate)
    filter_taps = jnp.einsum("mc,mkc->kc", coefficient, powers, precision=highest)
    offsets = jnp.arange(sub_len)[:, None] - jnp.arange(sub_len)[None, :]
    toeplitz = jnp.where(
        (offsets >= 0)[:, :, None], filter_taps[jnp.clip(offsets, 0, sub_len - 1)], 0.0
    )
    local_part = jnp.einsum("tsc,bsc->btc", toeplitz, pieces, precision=highest)
    ends = jnp.einsum("msc,bsc->bmc", powers[:, ::-1, :], pieces, precision=highest)
    sub_index = jnp.arange(sub_count)
    sub_gap = sub_index[:, None] - 1 - sub_index[None, :]
    gap_float = jnp.maximum(sub_gap, 0).astype(jnp.float32)
    within = jnp.where(
        (sub_gap >= 0)[:, :, None, None],
        jnp.exp(-(rate * sub_len)[None, None] * gap_float[:, :, None, None]),
        0.0,
    )
    inner = jnp.einsum("bamc,amc->bmc", within, ends, precision=highest)
    sub_decay = jnp.exp(-rate * sub_len)
    total_end = sub_decay * inner[-1] + ends[-1]
    dev_decay = jnp.exp(-rate * tok_rows)
    prefix = carried_in(
        (dev_decay, total_end),
        "ctx",
        compose,
        (jnp.ones_like(dev_decay), jnp.zeros_like(total_end)),
    )
    entering = prefix[1]
    start_powers = jnp.exp(-(rate * sub_len)[None] * sub_index.astype(jnp.float32)[:, None, None])
    arriving = inner + start_powers * entering[None]
    reach = coefficient[:, None, :] * powers * jnp.exp(-rate)[:, None, :]
    carried = jnp.einsum("mtc,bmc->btc", reach, arriving, precision=highest)
    conv = (local_part + carried).reshape(tok_rows, chan_count) + skip[None, :] * signal
    gated = (q_proj.astype(jnp.float32) * conv).astype(jnp.bfloat16)
    full_gated = lax.all_gather(gated, "ch", axis=1, tiled=True)
    mixed = jnp.dot(
        full_gated,
        lax.all_gather(w_out, "ctx", axis=0, tiled=True),
        preferred_element_type=jnp.float32,
    )
    return mixed.astype(jnp.bfloat16)


def solution(mesh):
    placed = (
        P("ctx", "ch"),
        P("ctx", "ch"),
        P("ctx", "ch"),
        P(None, "ch"),
        P(None, "ch"),
        P("ch"),
        P("ctx", "ch"),
    )
    return jax.shard_map(
        body, mesh=mesh, in_specs=placed, out_specs=P("ctx", "ch"), check_vma=False
    )
```

profile of v0, /device:TPU:32, one launch (start us, length us, event | category | flops | bytes accessed | tf_op | source)
XLA Modules:
  0.0 568.6 jit_solution(16598735904272384695)
XLA Ops:
  6.7 1.1 convert_multiply_fusion
  7.8 0.4 copy.49
  8.2 0.8 multiply_negate_fusion
  9.1 3.6 multiply_exponential_fusion
  12.7 7.3 %rev.3 = f32[16,64,512]{1,0,2:T(8,128)} reverse(f32[16,64,512]{1,0,2:T(8,128)} %multiply_exponential_fusion), dimensions={1} | reverse | bytes 4194304 | tf_op jit(solution)/shard_map/rev | solution.py:40
  20.0 8.4 %fusion.23 = f32[512,4,16]{2,1,0:T(4,128)S(1)} fusion(f32[4,64,512]{1,0,2:T(4,128)S(1)} %copy.49, f32[16,64,512]{1,0,2:T(8,128)} %rev.3), kind=kOutput, calls=%fused_computation.43 | convolution fusion | flops 25165824 | bytes 2752512 | tf_op jit(solution)/shard_map/msc,bsc->bmc/dot_general | solution.py:40
  28.9 0.7 negate_exponential_fusion
  29.6 0.7 all-gather.13.cloned.1.call-update
  30.5 0.8 copy.52
  31.5 6.0 %multiply_reduce_fusion = f32[512,64]{1,0:T(8,128)S(1)} fusion(f32[512,16]{1,0:T(8,128)S(1)} %copy.71, f32[64]{0:T(128)S(1)} %iota_convert_fusion.1, f32[16,512]{0,1:T(8,128)S(1)} %copy.47), kind=kLoop, calls=%fused_computation.7 | loop fusion | flops 1540096 | bytes 196864
  37.7 16.8 %gather_fusion = f32[4096,512]{1,0:T(8,128)} fusion(f32[64,512]{1,0:T(8,128)S(1)} %bitcast.54, s32[4096]{0:T(1024)S(1)} %broadcast_clamp_fusion), kind=kCustom, calls=%fused_computation | custom fusion | bytes 16793600 | tf_op jit(solution)/shard_map/gather | solution.py:37
  54.5 16.3 %copy.48 = f32[64,64,512]{1,0,2:T(8,128)} copy(f32[64,64,512]{2,1,0:T(8,128)} %bitcast.55) | data formatting | bytes 16777216 | tf_op jit(solution)/shard_map/gather | solution.py:37
  70.8 0.8 copy.53
  71.7 29.0 %fusion = f32[512,4,64]{2,1,0:T(4,128)S(1)} fusion(f32[4,64,512]{1,0,2:T(4,128)S(1)} %copy.49, f32[64,64,512]{1,0,2:T(8,128)} %copy.48, pred[64,64]{1,0:T(8,128)(4,1)S(1)} %subtract_compare_fusion), kind=kOutput, calls=%fused_computation.3 | convolution fusion | flops 102760448 | bytes 9441280 | tf_op jit(solution)/shard_map/tsc,bsc->btc/dot_general | solution.py:39
  100.7 74.2 %all-gather.11.cloned.1.call-done = f32[1024,512]{1,0:T(8,128)} async-done(((f32[16,512]{1,0:T(8,128)}), f32[1024,512]{1,0:T(8,128)}) %all-gather.11.cloned.1.call-update) | async-done | bytes 2097168 | tf_op jit(solution)/shard_map/all_gather | solution.py:9
  174.9 139.8 %all-gather.13.cloned.1.call-done = f32[1024,512]{1,0:T(8,128)} async-done(((f32[16,512]{1,0:T(8,128)}), f32[1024,512]{1,0:T(8,128)}) %all-gather.13.cloned.1.call-update) | async-done | bytes 2097168 | tf_op jit(solution)/shard_map/all_gather | solution.py:9
  314.7 0.8 while.12
  314.7 0.8 bitcast_add_fusion.3
  316.0 8.4 %fusion.14 = f32[4,64,512]{1,0,2:T(4,128)S(1)} fusion(f32[512,4,64]{2,1,0:T(4,128)S(1)} %fusion, f32[4,16,512]{1,0,2:T(4,128)S(1)} %copy.54, f32[16,512]{0,1:T(8,128)} %copy.53, f32[16,512]{0,1:T(8,128)} %copy.52, f32[64]{0:T(128)S(1)} %iota_convert_fusion.1, f32[16,512]{0,1:T(8,128)S(1)} %copy.47), kind=kOutput, calls=%fused_computation.17 | convolution fusion | flops 26869760 | bytes 1278208 | tf_op jit(solution)/shard_map/mtc,bmc->btc/dot_general | solution.py:63
  324.9 2.0 fusion.18
  326.9 0.5 all-gather.9.cloned.1.call-update
  327.4 74.4 %all-gather.7.cloned.1.call-done = bf16[256,4096]{1,0:T(8,128)(2,1)} async-done(((bf16[256,512]{1,0:T(8,128)(2,1)}), bf16[256,4096]{1,0:T(8,128)(2,1)}) %all-gather.7.cloned.1.call-update) | async-done | bytes 2097168 | tf_op jit(solution)/shard_map/all_gather | solution.py:66
  401.8 154.3 %all-gather.9.cloned.1.call-done = bf16[4096,768]{1,0:T(8,128)(2,1)} async-done(((bf16[64,768]{1,0:T(8,128)(2,1)}), bf16[4096,768]{1,0:T(8,128)(2,1)}) %all-gather.9.cloned.1.call-update) | async-done | bytes 6291472 | tf_op jit(solution)/shard_map/all_gather | solution.py:69
  556.2 6.0 %convolution_convert_fusion = bf16[256,768]{1,0:T(8,128)(2,1)} fusion(bf16[256,4096]{1,0:T(8,128)(2,1)} %all-gather.7.cloned.1.call-done, bf16[4096,768]{1,0:T(8,128)(2,1)} %all-gather.9.cloned.1.call-done), kind=kOutput, calls=%fused_computation.18 | convolution fusion | flops 1610809344 | bytes 8781824 | tf_op jit(solution)/shard_map/dot_general | solution.py:67
  (30 shorter events, 2.3 us)
Async XLA Ops:
  6.5 168.4 %all-gather.11.cloned.1.call-start = ((), (), s32[]{:S(2)}) async-start(), calls=%async_computation.2 | async-start | bytes 2129920 | tf_op jit(solution)/shard_map/all_gather | solution.py:9
  20.0 8.9 %copy-start = (f32[16,512]{1,0:T(8,128)S(1)}, f32[16,512]{1,0:T(8,128)}, u32[]{:S(2)}) copy-start(f32[16,512]{1,0:T(8,128)} %param.13) | copy-start | bytes 98308
  20.0 8.9 %copy-start.1 = (f32[16,512]{1,0:T(8,128)S(1)}, f32[16,512]{1,0:T(8,128)}, u32[]{:S(2)}) copy-start(f32[16,512]{1,0:T(8,128)} %param.12) | copy-start | bytes 98308
  29.5 285.2 %all-gather.13.cloned.1.call-start = ((), (), s32[]{:S(2)}) async-start(), calls=%async_computation.3 | async-start | bytes 2129920 | tf_op jit(solution)/shard_map/all_gather | solution.py:9
  30.3 371.5 %all-gather.7.cloned.1.call-start = ((), (), s32[]{:S(2)}) async-start(), calls=%async_computation | async-start | bytes 2359296 | tf_op jit(solution)/shard_map/all_gather | solution.py:66
  316.0 8.8 %copy-start.2 = (f32[512]{0:T(512)S(1)}, f32[512]{0:T(512)}, u32[]{:S(2)}) copy-start(f32[512]{0:T(512)} %param.14) | copy-start | bytes 6148
  326.8 229.3 %all-gather.9.cloned.1.call-start = ((), (), s32[]{:S(2)}) async-start(), calls=%async_computation.1 | async-start | bytes 6389760 | tf_op jit(solution)/shard_map/all_gather | solution.py:69
Sparse Core Ops, SparseCore 0:
  29.7 145.1 all-gather.10
  177.8 136.8 all-gather.12
  326.9 74.8 all-gather.6
  404.6 151.4 all-gather.8
where the time goes:
time: 574 us; the launch traced here: 569 us
  waiting for transfers between devices  444 us (77%)
  matrix products  51.7 us (9%)
  local copies, waits for them, and re-layouts  44 us (8%)
  other arithmetic  15.3 us (3%)
  between operations  13.3 us (2%)
    all_gather x2, waiting for transfers between devices, carried_in(): gathered = jax.tree.map(lambda a: lax.all_gather(a, axis), part)  214 us
    all_gather x1, waiting for transfers between devices, body(): lax.all_gather(w_out, 'ctx', axis=0, tiled=True)  154 us
    all_gather x1, waiting for transfers between devices, body(): full_gated = lax.all_gather(gated, 'ch', axis=1, tiled=True)  74.4 us
    gather x2, local copies, waits for them, and re-layouts, body(): filter_taps[jnp.clip(offsets, 0, sub_len - 1)]  33.1 us
    dot_general x1, matrix products, body(): local_part = jnp.einsum('tsc,bsc->btc', toeplitz, pieces, precision=highest)  29 us
  transfers between devices with their start and end apart: 4, of which 4 were waited for; matrix products, arithmetic and copies ran while one was open for 12% of the time, Pallas kernels for 0%

commit v1 on v0

--- a/solution.py
+++ b/solution.py
@@ -66,7 +66,9 @@
     full_gated = lax.all_gather(gated, "ch", axis=1, tiled=True)
     mixed = jnp.dot(
         full_gated,
-        lax.all_gather(w_out, "ctx", axis=0, tiled=True),
+        jnp.concatenate(
+            lax.all_to_all(jnp.stack([w_out] * lax.axis_size("ctx")), "ctx", 0, 0), axis=0
+        ),
         preferred_element_type=jnp.float32,
     )
     return mixed.astype(jnp.bfloat16)

time: 574 us -> 497 us (0.87)
  the two profiles are of different devices: /device:TPU:32 before, /device:TPU:1 now
where the time goes in v1:
time: 497 us; the launch traced here: 492 us
  waiting for transfers between devices  346 us (70%)
  matrix products  51.7 us (10%)
  local copies, waits for them, and re-layouts  48.2 us (10%)
  starting transfers between devices  19.8 us (4%)
  between operations  13.3 us (3%)
  other arithmetic  12.7 us (3%)
    all_gather x2, waiting for transfers between devices, carried_in(): gathered = jax.tree.map(lambda a: lax.all_gather(a, axis), part)  259 us
    all_gather x1, waiting for transfers between devices, body(): full_gated = lax.all_gather(gated, 'ch', axis=1, tiled=True)  86.3 us
    gather x2, local copies, waits for them, and re-layouts, body(): filter_taps[jnp.clip(offsets, 0, sub_len - 1)]  33 us
    dot_general x1, matrix products, body(): local_part = jnp.einsum('tsc,bsc->btc', toeplitz, pieces, precision=highest)  29 us
    all_to_all x1, starting transfers between devices, body(): lax.all_to_all(jnp.stack([w_out] * lax.axis_size('ctx')), 'ctx', 0, 0)  19.5 us
  transfers between devices with their start and end apart: 4, of which 3 were waited for; matrix products, arithmetic and copies ran while one was open for 21% of the time, Pallas kernels for 0%

profile of v1, /device:TPU:1, one launch (start us, length us, event | category | flops | bytes accessed | tf_op | source)
XLA Modules:
  0.0 492.0 jit_solution(16667361858153339948)
XLA Ops:
  6.5 4.4 stack.2
  10.9 19.5 %all-to-all-start = ((bf16[64,64,768]{2,1,0:T(8,128)(2,1)}), bf16[64,64,768]{2,1,0:T(8,128)(2,1)}, u32[]{:S(2)}, u32[]{:S(2)}) async-start(bf16[64,64,768]{2,1,0:T(8,128)(2,1)} %stack.2), calls=%async_computation | async-start | bytes 12582912 | tf_op jit(solution)/shard_map/all_to_all | solution.py:70
  30.5 0.4 copy.49
  31.1 3.6 multiply_exponential_fusion
  34.7 7.3 %rev.3 = f32[16,64,512]{1,0,2:T(8,128)} reverse(f32[16,64,512]{1,0,2:T(8,128)} %multiply_exponential_fusion), dimensions={1} | reverse | bytes 4194304 | tf_op jit(solution)/shard_map/rev | solution.py:40
  41.9 8.4 %fusion.23 = f32[512,4,16]{2,1,0:T(4,128)S(1)} fusion(f32[4,64,512]{1,0,2:T(4,128)S(1)} %copy.49, f32[16,64,512]{1,0,2:T(8,128)} %rev.3), kind=kOutput, calls=%fused_computation.43 | convolution fusion | flops 25165824 | bytes 2752512 | tf_op jit(solution)/shard_map/msc,bsc->bmc/dot_general | solution.py:40
  50.3 0.3 copy.73
  51.0 0.6 negate_exponential_fusion
  51.7 0.7 all-gather.10.cloned.1.call-update
  52.4 0.2 all-gather.6.cloned.1.call-start
  52.6 0.8 copy.52
  53.6 6.0 %multiply_reduce_fusion = f32[512,64]{1,0:T(8,128)S(1)} fusion(f32[512,16]{1,0:T(8,128)S(1)} %copy.71, f32[64]{0:T(128)S(1)} %iota_convert_fusion.1, f32[16,512]{0,1:T(8,128)S(1)} %copy.47), kind=kLoop, calls=%fused_computation.7 | loop fusion | flops 1540096 | bytes 196864
  59.8 16.8 %gather_fusion = f32[4096,512]{1,0:T(8,128)} fusion(f32[64,512]{1,0:T(8,128)S(1)} %bitcast.55, s32[4096]{0:T(1024)S(1)} %broadcast_clamp_fusion), kind=kCustom, calls=%fused_computation | custom fusion | bytes 16793600 | tf_op jit(solution)/shard_map/gather | solution.py:37
  76.6 16.2 %copy.48 = f32[64,64,512]{1,0,2:T(8,128)} copy(f32[64,64,512]{2,1,0:T(8,128)} %bitcast.56) | data formatting | bytes 16777216 | tf_op jit(solution)/shard_map/gather | solution.py:37
  92.8 0.8 copy.53
  93.7 29.0 %fusion = f32[512,4,64]{2,1,0:T(4,128)S(1)} fusion(f32[4,64,512]{1,0,2:T(4,128)S(1)} %copy.49, f32[64,64,512]{1,0,2:T(8,128)} %copy.48, pred[64,64]{1,0:T(8,128)(4,1)S(1)} %subtract_compare_fusion), kind=kOutput, calls=%fused_computation.3 | convolution fusion | flops 102760448 | bytes 9441280 | tf_op jit(solution)/shard_map/tsc,bsc->btc/dot_general | solution.py:39
  122.6 103.9 %all-gather.8.cloned.1.call-done = f32[1024,512]{1,0:T(8,128)} async-done(((f32[16,512]{1,0:T(8,128)}), f32[1024,512]{1,0:T(8,128)}) %all-gather.8.cloned.1.call-update) | async-done | bytes 2097168 | tf_op jit(solution)/shard_map/all_gather | solution.py:9
  226.5 155.3 %all-gather.10.cloned.1.call-done = f32[1024,512]{1,0:T(8,128)} async-done(((f32[16,512]{1,0:T(8,128)}), f32[1024,512]{1,0:T(8,128)}) %all-gather.10.cloned.1.call-update) | async-done | bytes 2097168 | tf_op jit(solution)/shard_map/all_gather | solution.py:9
  381.9 0.4 copy.54
  382.3 8.4 %fusion.14 = f32[4,64,512]{1,0,2:T(4,128)S(1)} fusion(f32[512,4,64]{2,1,0:T(4,128)S(1)} %fusion, f32[4,16,512]{1,0,2:T(4,128)S(1)} %copy.54, f32[16,512]{0,1:T(8,128)} %copy.53, f32[16,512]{0,1:T(8,128)} %copy.52, f32[64]{0:T(128)S(1)} %iota_convert_fusion.1, f32[16,512]{0,1:T(8,128)S(1)} %copy.47), kind=kOutput, calls=%fused_computation.17 | convolution fusion | flops 26869760 | bytes 1278208 | tf_op jit(solution)/shard_map/mtc,bmc->btc/dot_general | solution.py:63
  390.8 0.3 copy.55
  391.1 2.0 fusion.18
  393.1 86.3 %all-gather.6.cloned.1.call-done = bf16[256,4096]{1,0:T(8,128)(2,1)} async-done(((bf16[256,512]{1,0:T(8,128)(2,1)}), bf16[256,4096]{1,0:T(8,128)(2,1)}) %all-gather.6.cloned.1.call-update) | async-done | bytes 2097168 | tf_op jit(solution)/shard_map/all_gather | solution.py:66
  479.5 6.0 %convolution_convert_fusion = bf16[256,768]{1,0:T(8,128)(2,1)} fusion(bf16[256,4096]{1,0:T(8,128)(2,1)} %all-gather.6.cloned.1.call-done, bf16[4096,768]{1,0:T(8,128)(2,1)} %bitcast.20), kind=kOutput, calls=%fused_computation.18 | convolution fusion | flops 1610809344 | bytes 8781824 | tf_op jit(solution)/shard_map/dot_general | solution.py:67
  (33 shorter events, 1.1 us)
Async XLA Ops:
  10.9 19.5 %copy-start = (bf16[256,512]{1,0:T(8,128)(2,1)S(1)}, bf16[256,512]{1,0:T(8,128)(2,1)}, u32[]{:S(2)}) copy-start(bf16[256,512]{1,0:T(8,128)(2,1)} %param.11) | copy-start | bytes 786436
  10.9 19.5 %copy-start.1 = (bf16[256,512]{1,0:T(8,128)(2,1)S(1)}, bf16[256,512]{1,0:T(8,128)(2,1)}, u32[]{:S(2)}) copy-start(bf16[256,512]{1,0:T(8,128)(2,1)} %param.10) | copy-start | bytes 786436
  10.9 20.0 %copy-start.2 = (f32[16,512]{1,0:T(8,128)S(1)}, f32[16,512]{1,0:T(8,128)}, u32[]{:S(2)}) copy-start(f32[16,512]{1,0:T(8,128)} %param.13) | copy-start | bytes 98308
  10.9 468.5 %all-to-all-start = ((bf16[64,64,768]{2,1,0:T(8,128)(2,1)}), bf16[64,64,768]{2,1,0:T(8,128)(2,1)}, u32[]{:S(2)}, u32[]{:S(2)}) async-start(bf16[64,64,768]{2,1,0:T(8,128)(2,1)} %stack.2), calls=%async_computation | async-start | bytes 12582912 | tf_op jit(solution)/shard_map/all_to_all | solution.py:70
  30.4 196.1 %all-gather.8.cloned.1.call-start = ((), (), s32[]{:S(2)}) async-start(), calls=%async_computation.2 | async-start | bytes 2129920 | tf_op jit(solution)/shard_map/all_gather | solution.py:9
  41.9 9.1 %copy-start.3 = (f32[16,512]{1,0:T(8,128)S(1)}, f32[16,512]{1,0:T(8,128)}, u32[]{:S(2)}) copy-start(f32[16,512]{1,0:T(8,128)} %param.12) | copy-start | bytes 98308
  51.7 330.2 %all-gather.10.cloned.1.call-start = ((), (), s32[]{:S(2)}) async-start(), calls=%async_computation.3 | async-start | bytes 2129920 | tf_op jit(solution)/shard_map/all_gather | solution.py:9
  52.4 427.1 %all-gather.6.cloned.1.call-start = ((), (), s32[]{:S(2)}) async-start(), calls=%async_computation.1 | async-start | bytes 2359296 | tf_op jit(solution)/shard_map/all_gather | solution.py:66
  382.3 8.8 %copy-start.4 = (f32[512]{0:T(512)S(1)}, f32[512]{0:T(512)}, u32[]{:S(2)}) copy-start(f32[512]{0:T(512)} %param.14) | copy-start | bytes 6148
Sparse Core Ops, SparseCore 0:
  51.8 174.6 all-gather.7
  229.4 152.3 all-gather.9
  393.2 86.1 all-gather.5
